TPU v7x, 32 devices: a whole 2x2x4 slice. The times are simulated.
32 devices in a mesh: seq: 16 (over z, x, core), head: 2 (over y).
Axes of the slice: x: 2, y: 2, z: 4, core: 2. Of those that a mesh axis runs over, the one named last changes fastest.
Arguments:
- queries: bfloat16 [2, 1024, 4096], P(None, ('seq', 'head')), may hold values from -6 to 6
- keys: bfloat16 [2, 1024, 4096], P(None, ('seq', 'head')), may hold values from -6 to 6
- values: bfloat16 [2, 1024, 4096], P(None, ('seq', 'head')), may hold values from -6 to 6
- rates: bfloat16 [2, 1024, 8], P(None, ('seq', 'head')), may hold values from 0.049804688 to 1
- fast_init: float32 [8, 3, 512, 256], P('head', None, 'seq'), may hold values from -0.25 to 0.25
Outputs:
- outputs: bfloat16 [2, 1024, 4096], P(None, 'seq', 'head')
All inputs are finite; a program needn't handle non-finite values.
Results may differ from a plain program's by a relative error of at most 0.0085.
Values may be sent and summed in bfloat16 or wider, within the bound.
No kernel may reach another device: no remote copies, remote signals or barrier semaphores. Data moves between devices by JAX's collectives and lax.ppermute only.
A program may use at most 64 MiB of HBM per device.

v0:
```python
import jax
import jax.numpy as jnp
from jax import lax
from jax.sharding import PartitionSpec as P

EPSILON = 1e-06
COEF_A = 3.4445
COEF_B = -4.775
COEF_C = 2.0315
LEARNING_STEP = 0.5
FULL_PRECISION = lax.Precision.HIGHEST


def silu_parts(gate_pre):
    sigmoid_value = jax.nn.sigmoid(gate_pre)
    return (gate_pre * sigmoid_value, sigmoid_value * (1.0 + gate_pre * (1.0 - sigmoid_value)))


def local_gram(weight_matrices):
    return jnp.einsum("hmrf,hmrg->hmfg", weight_matrices, weight_matrices, precision=FULL_PRECISION)


def newton_schulz(gradients, gram_fn):
    gram_matrix = gram_fn(gradients)
    norm_value = jnp.sqrt(jnp.trace(gram_matrix, axis1=2, axis2=3)) + EPSILON
    current_weights = gradients / norm_value[:, :, None, None]
    gram_matrix = gram_matrix / (norm_value * norm_value)[:, :, None, None]
    identity = jnp.eye(gram_matrix.shape[-1], dtype=gram_matrix.dtype)
    for sweeps in range(2):
        if sweeps > 0:
            gram_matrix = gram_fn(current_weights)
        square = jnp.einsum("hmfg,hmgk->hmfk", gram_matrix, gram_matrix, precision=FULL_PRECISION)
        polynomial_update = COEF_A * identity + COEF_B * gram_matrix + COEF_C * square
        current_weights = jnp.einsum(
            "hmrf,hmfg->hmrg", current_weights, polynomial_update, precision=FULL_PRECISION
        )
    return current_weights


def local(queries, keys, values, rates, fast_init):
    weights = lax.all_gather(fast_init, "seq", axis=2, tiled=True)
    head_count = weights.shape[0]
    head_size = weights.shape[2]
    results = []
    for group_index in range(queries.shape[0]):
        query_flat, key_flat, value_flat, rate_rows = (
            lax.all_to_all(queries[group_index], "head", split_axis=1, concat_axis=0, tiled=True),
            lax.all_to_all(keys[group_index], "head", split_axis=1, concat_axis=0, tiled=True),
            lax.all_to_all(values[group_index], "head", split_axis=1, concat_axis=0, tiled=True),
            lax.all_to_all(rates[group_index], "head", split_axis=1, concat_axis=0, tiled=True),
        )
        row_count = query_flat.shape[0]
        query_rows = query_flat.reshape(row_count, head_count, head_size)
        key_rows = key_flat.reshape(row_count, head_count, head_size)
        value_rows = value_flat.reshape(row_count, head_count, head_size)
        low = weights.astype(jnp.bfloat16)
        gate_pre = jnp.einsum(
            "rhd,hdf->rhf", key_rows, low[:, 0], preferred_element_type=jnp.float32
        )
        up_proj = jnp.einsum(
            "rhd,hdf->rhf", key_rows, low[:, 1], preferred_element_type=jnp.float32
        )
        activated_hidden, slope_value = silu_parts(gate_pre)
        hidden = (activated_hidden * up_proj).astype(jnp.bfloat16)
        out_grad = (
            -(rate_rows.astype(jnp.float32)[:, :, None] * value_rows.astype(jnp.float32))
        ).astype(jnp.bfloat16)
        hidden_grad = jnp.einsum(
            "rhd,hdf->rhf", out_grad, low[:, 2], preferred_element_type=jnp.float32
        )
        gate_grad = (hidden_grad * up_proj * slope_value).astype(jnp.bfloat16)
        up_grad = (hidden_grad * activated_hidden).astype(jnp.bfloat16)
        gradients = jnp.stack(
            [
                jnp.einsum("rhd,rhf->hdf", key_rows, gate_grad, preferred_element_type=jnp.float32),
                jnp.einsum("rhd,rhf->hdf", key_rows, up_grad, preferred_element_type=jnp.float32),
                jnp.einsum("rhd,rhf->hdf", out_grad, hidden, preferred_element_type=jnp.float32),
            ],
            axis=1,
        )
        total_grad = lax.psum(gradients, "seq")
        update = newton_schulz(total_grad, local_gram)
        weights = weights - LEARNING_STEP * update
        low = weights.astype(jnp.bfloat16)
        query_gate = jnp.einsum(
            "rhd,hdf->rhf", query_rows, low[:, 0], preferred_element_type=jnp.float32
        )
        query_up = jnp.einsum(
            "rhd,hdf->rhf", query_rows, low[:, 1], preferred_element_type=jnp.float32
        )
        query_act, unused_slope = silu_parts(query_gate)
        query_hidden = (query_act * query_up).astype(jnp.bfloat16)
        result = jnp.einsum(
            "rhf,hdf->rhd", query_hidden, low[:, 2], preferred_element_type=jnp.float32
        )
        results.append(result.astype(jnp.bfloat16).reshape(row_count, head_count * head_size))
    return jnp.stack(results)


def solution(mesh):
    return jax.shard_map(
        local,
        mesh=mesh,
        in_specs=(
            P(None, ("seq", "head"), None),
            P(None, ("seq", "head"), None),
            P(None, ("seq", "head"), None),
            P(None, ("seq", "head"), None),
            P("head", None, "seq", None),
        ),
        out_specs=P(None, "seq", "head"),
        check_vma=False,
    )
```

profile of v0, /device:TPU:0, one launch (start us, length us, event | category | flops | bytes accessed | tf_op | source)
XLA Modules:
  0.0 496.7 jit_solution(14485534307048518920)
XLA Ops:
  9.7 4.3 all-to-all-start
  17.7 3.5 all-to-all-start.2
  22.2 4.1 all-to-all-done.2
  26.4 3.4 all-to-all-start.1
  30.1 4.8 all-to-all-done.1
  35.5 38.2 %all-gather.2.cloned.1.call-done = f32[4,3,512,256]{3,2,0,1:T(8,128)} async-done(((f32[4,3,32,256]{3,2,0,1:T(8,128)}), f32[4,3,512,256]{3,2,0,1:T(8,128)}) %all-gather.2.cloned.1.call-update) | async-done | bytes 6291472 | tf_op jit(solution)/shard_map/all_gather | solution.py:41
  73.7 3.1 convert_element_type.105
  79.3 3.3 pad_maximum_fusion
  82.6 3.2 all-to-all-start.4
  89.5 3.4 all-to-all-start.5
  93.0 5.1 %all-to-all-done.5 = bf16[32,2,2048]{2,0,1:T(8,128)(2,1)S(1)} async-done(((bf16[32,2,2048]{2,0,1:T(8,128)(2,1)}), bf16[32,2,2048]{2,0,1:T(8,128)(2,1)S(1)}, u32[]{:S(2)}, u32[]{:S(2)}) %all-to-all-start.5) | async-done | bytes 262176 | tf_op jit(solution)/shard_map/all_to_all | solution.py:49
  98.1 3.4 all-to-all-start.6
  102.2 4.5 all-to-all-done.6
  108.5 112.3 %all-reduce.3.cloned.1.call-done = f32[4,3,512,256]{2,3,0,1:T(8,128)} async-done(((f32[4,3,512,256]{2,3,0,1:T(8,128)}), f32[4,3,512,256]{2,3,0,1:T(8,128)}) %all-reduce.3.cloned.1.call-update) | async-done | bytes 6291472 | tf_op jit(solution)/shard_map/psum | solution.py:81
  220.8 19.0 %select_reduce_fusion.1 = (f32[4,3]{1,0:T(4,128)S(1)}, f32[4,3,256,256]{3,2,1,0:T(8,128)}) fusion(pred[256,256]{1,0:T(8,128)(4,1)S(1)} %iota_compare_fusion, f32[4,3,512,256]{2,3,0,1:T(8,128)} %all-reduce.3.cloned.1.call-done), kind=kOutput, calls=%fused_computation.31 | convolution fusion | flops 4833411072 | bytes 9502768 | tf_op jit(solution)/shard_map/hmrf,hmrg->hmfg/dot_general | solution.py:20
  239.9 6.4 %fusion.36 = f32[4,3,256,256]{3,2,1,0:T(8,128)S(1)} fusion(f32[4,3,256,256]{3,2,1,0:T(8,128)} %get-tuple-element.18, f32[4,3]{1,0:T(4,128)S(1)} %get-tuple-element.15), kind=kOutput, calls=%fused_computation.46 | convolution fusion | flops 2416705536 | bytes 6291504 | tf_op jit(solution)/shard_map/hmfg,hmgk->hmfk/dot_general | solution.py:32
  246.4 10.8 %fusion.2 = f32[4,3,512,256]{3,2,1,0:T(8,128)S(1)} fusion(f32[4,3,256,256]{3,2,1,0:T(8,128)S(1)} %fusion.36, f32[256,256]{1,0:T(8,128)S(1)} %broadcast_select_fusion, f32[4,3,256,256]{3,2,1,0:T(8,128)S(1)} %copy-done.1, f32[4,3]{1,0:T(4,128)S(1)} %get-tuple-element.15, f32[4,3,512,256]{2,3,0,1:T(8,128)S(1)} %bitcast.117, f32[4,3]{0,1:T(4,128)S(1)} %copy.76), kind=kOutput, calls=%fused_computation.4 | convolution fusion | flops 4837343232 | bytes 19136608 | tf_op jit(solution)/shard_map/hmrf,hmfg->hmrg/dot_general | solution.py:34
  257.2 10.6 %fusion.101 = f32[4,3,256,256]{3,2,1,0:T(8,128)S(1)} fusion(f32[4,3,512,256]{3,2,1,0:T(8,128)S(1)} %fusion.2), kind=kOutput, calls=%fused_computation.145 | convolution fusion | flops 4831838208 | bytes 9437184 | tf_op jit(solution)/shard_map/hmrf,hmrg->hmfg/dot_general | solution.py:20
  267.9 3.9 multiply_add_fusion.1
  271.8 8.1 %fusion.100 = (bf16[4,3,512,256]{3,2,0,1:T(8,128)(2,1)S(1)}, f32[4,3,512,256]{3,2,0,1:T(8,128)}) fusion(f32[4,3,512,256]{3,2,0,1:T(8,128)S(1)} %bitcast.115, f32[4,3,256,256]{3,2,1,0:T(8,128)S(1)} %multiply_add_fusion.1, f32[4,3,512,256]{3,2,1,0:T(8,128)S(1)} %fusion.2), kind=kOutput, calls=%fused_computation.144 | convolution fusion | flops 4836556800 | bytes 25165824 | tf_op jit(solution)/shard_map/hmrf,hmfg->hmrg/dot_general | solution.py:34
  282.6 3.3 pad_maximum_fusion.1
  291.5 4.1 all-to-all-start.3
  300.9 4.1 all-to-all-start.7
  306.8 3.4 all-to-all-done.7
  318.4 107.0 %all-reduce.5.cloned.1.call-done = f32[4,3,512,256]{2,3,0,1:T(8,128)} async-done(((f32[4,3,512,256]{2,3,0,1:T(8,128)}), f32[4,3,512,256]{2,3,0,1:T(8,128)}) %all-reduce.5.cloned.1.call-update) | async-done | bytes 6291472 | tf_op jit(solution)/shard_map/psum | solution.py:81
  425.5 18.8 %select_reduce_fusion = (f32[4,3]{1,0:T(4,128)S(1)}, f32[4,3,256,256]{3,2,1,0:T(8,128)}) fusion(pred[256,256]{1,0:T(8,128)(4,1)S(1)} %iota_compare_fusion, f32[4,3,512,256]{2,3,0,1:T(8,128)} %all-reduce.5.cloned.1.call-done), kind=kOutput, calls=%fused_computation.24 | convolution fusion | flops 4833411072 | bytes 9502768 | tf_op jit(solution)/shard_map/hmrf,hmrg->hmfg/dot_general | solution.py:20
  444.4 6.7 %fusion.37 = f32[4,3,256,256]{3,2,1,0:T(8,128)S(1)} fusion(f32[4,3,256,256]{3,2,1,0:T(8,128)} %get-tuple-element.22, f32[4,3]{1,0:T(4,128)S(1)} %get-tuple-element.13), kind=kOutput, calls=%fused_computation.47 | convolution fusion | flops 2416705536 | bytes 6291504 | tf_op jit(solution)/shard_map/hmfg,hmgk->hmfk/dot_general | solution.py:32
  451.1 11.4 %fusion = f32[4,3,512,256]{3,2,1,0:T(8,128)S(1)} fusion(f32[4,3,256,256]{3,2,1,0:T(8,128)S(1)} %fusion.37, f32[256,256]{1,0:T(8,128)S(1)} %broadcast_select_fusion, f32[4,3,256,256]{3,2,1,0:T(8,128)S(1)} %copy-done, f32[4,3]{1,0:T(4,128)S(1)} %get-tuple-element.13, f32[4,3,512,256]{2,3,0,1:T(8,128)S(1)} %bitcast.119, f32[4,3]{0,1:T(4,128)S(1)} %copy.97), kind=kOutput, calls=%fused_computation.2 | convolution fusion | flops 4837343232 | bytes 19136608 | tf_op jit(solution)/shard_map/hmrf,hmfg->hmrg/dot_general | solution.py:34
  462.6 10.8 %fusion.102 = f32[4,3,256,256]{3,2,1,0:T(8,128)S(1)} fusion(f32[4,3,512,256]{3,2,1,0:T(8,128)S(1)} %fusion), kind=kOutput, calls=%fused_computation.146 | convolution fusion | flops 4831838208 | bytes 9437184 | tf_op jit(solution)/shard_map/hmrf,hmrg->hmfg/dot_general | solution.py:20
  473.4 4.1 multiply_add_fusion
  477.6 6.5 %subtract_convert_fusion = bf16[4,3,512,256]{3,2,0,1:T(8,128)(2,1)S(1)} fusion(f32[4,3,512,256]{3,2,0,1:T(8,128)S(1)} %bitcast.113, f32[4,3,256,256]{3,2,1,0:T(8,128)S(1)} %multiply_add_fusion, f32[4,3,512,256]{3,2,1,0:T(8,128)S(1)} %fusion), kind=kOutput, calls=%fused_computation.14 | convolution fusion | flops 4836556800 | bytes 18874368 | tf_op jit(solution)/shard_map/hmrf,hmfg->hmrg/dot_general | solution.py:34
  485.2 2.4 fusion.39
  (100 shorter events, 44.4 us)
Async XLA Ops:
  6.5 14.7 %copy-start.5 = (bf16[2,32,4096]{2,1,0:T(8,128)(2,1)S(1)}, bf16[2,32,4096]{2,1,0:T(8,128)(2,1)}, u32[]{:S(2)}) copy-start(bf16[2,32,4096]{2,1,0:T(8,128)(2,1)} %param.7) | copy-start | bytes 1572868
  6.5 67.2 %all-gather.2.cloned.1.call-start = ((), (), s32[]{:S(2)}) async-start(), calls=%async_computation.8 | async-start | bytes 6684672 | tf_op jit(solution)/shard_map/all_gather | solution.py:41
  9.7 8.0 %all-to-all-start = ((bf16[32,2,4]{0,2,1:T(4,128)(2,1)}), bf16[32,2,4]{0,2,1:T(4,128)(2,1)S(1)}, u32[]{:S(2)}, u32[]{:S(2)}) async-start(bf16[32,2,4]{0,2,1:T(4,128)(2,1)} %bitcast), calls=%async_computation | async-start | bytes 4096 | tf_op jit(solution)/shard_map/all_to_all | solution.py:50
  17.7 8.6 %all-to-all-start.2 = ((bf16[32,2,2048]{2,0,1:T(8,128)(2,1)}), bf16[32,2,2048]{2,0,1:T(8,128)(2,1)S(1)}, u32[]{:S(2)}, u32[]{:S(2)}) async-start(bf16[32,2,2048]{2,0,1:T(8,128)(2,1)} %copy.67), calls=%async_computation.2 | async-start | bytes 524288 | tf_op jit(solution)/shard_map/all_to_all | solution.py:48
  26.4 8.6 %all-to-all-start.1 = ((bf16[32,2,2048]{2,0,1:T(8,128)(2,1)}), bf16[32,2,2048]{2,0,1:T(8,128)(2,1)S(1)}, u32[]{:S(2)}, u32[]{:S(2)}) async-start(bf16[32,2,2048]{2,0,1:T(8,128)(2,1)} %copy.65), calls=%async_computation.1 | async-start | bytes 524288 | tf_op jit(solution)/shard_map/all_to_all | solution.py:49
  29.8 191.0 %all-reduce.3.cloned.1.call-start = ((), (), s32[]{:S(2)}) async-start(), calls=%async_computation.9 | async-start | bytes 12582912 | tf_op jit(solution)/shard_map/psum | solution.py:81
  82.6 6.8 %all-to-all-start.4 = ((bf16[32,2,4]{0,2,1:T(4,128)(2,1)}), bf16[32,2,4]{0,2,1:T(4,128)(2,1)S(1)}, u32[]{:S(2)}, u32[]{:S(2)}) async-start(bf16[32,2,4]{0,2,1:T(4,128)(2,1)} %bitcast.23), calls=%async_computation.4 | async-start | bytes 4096 | tf_op jit(solution)/shard_map/all_to_all | solution.py:50
  89.5 8.6 %all-to-all-start.5 = ((bf16[32,2,2048]{2,0,1:T(8,128)(2,1)}), bf16[32,2,2048]{2,0,1:T(8,128)(2,1)S(1)}, u32[]{:S(2)}, u32[]{:S(2)}) async-start(bf16[32,2,2048]{2,0,1:T(8,128)(2,1)} %copy.86), calls=%async_computation.5 | async-start | bytes 524288 | tf_op jit(solution)/shard_map/all_to_all | solution.py:49
  98.1 8.6 %all-to-all-start.6 = ((bf16[32,2,2048]{2,0,1:T(8,128)(2,1)}), bf16[32,2,2048]{2,0,1:T(8,128)(2,1)S(1)}, u32[]{:S(2)}, u32[]{:S(2)}) async-start(bf16[32,2,2048]{2,0,1:T(8,128)(2,1)} %copy.88), calls=%async_computation.6 | async-start | bytes 524288 | tf_op jit(solution)/shard_map/all_to_all | solution.py:48
  101.5 324.0 %all-reduce.5.cloned.1.call-start = ((), (), s32[]{:S(2)}) async-start(), calls=%async_computation.10 | async-start | bytes 12582912 | tf_op jit(solution)/shard_map/psum | solution.py:81
  220.8 25.5 %slice-start.4 = ((s8[6291456]{0:T(1024)(128)(4,1)}), s8[2097152]{0:T(1024)(128)(4,1)S(1)}, s32[]{:S(2)}) async-start(s8[6291456]{0:T(1024)(128)(4,1)} %bitcast.116), calls=%async_computation.15 | async-start | bytes 4194304
  239.9 6.4 %slice-start.5 = ((s8[6291456]{0:T(1024)(128)(4,1)}), s8[4194304]{0:T(1024)(128)(4,1)S(1)}, s32[]{:S(2)}) async-start(s8[6291456]{0:T(1024)(128)(4,1)} %bitcast.116), calls=%async_computation.16 | async-start | bytes 8388608
  239.9 6.4 %copy-start.1 = (f32[4,3,256,256]{3,2,1,0:T(8,128)S(1)}, f32[4,3,256,256]{3,2,1,0:T(8,128)}, u32[]{:S(2)}) copy-start(f32[4,3,256,256]{3,2,1,0:T(8,128)} %get-tuple-element.18) | copy-start | bytes 9437188
  239.9 31.8 %slice-start.2 = ((s8[6291456]{0:T(1024)(128)(4,1)}), s8[4194304]{0:T(1024)(128)(4,1)S(1)}, s32[]{:S(2)}) async-start(s8[6291456]{0:T(1024)(128)(4,1)} %bitcast.114), calls=%async_computation.13 | async-start | bytes 8388608
  246.4 25.4 %slice-start.3 = ((s8[6291456]{0:T(1024)(128)(4,1)}), s8[2097152]{0:T(1024)(128)(4,1)S(1)}, s32[]{:S(2)}) async-start(s8[6291456]{0:T(1024)(128)(4,1)} %bitcast.114), calls=%async_computation.14 | async-start | bytes 4194304
  271.8 8.1 %copy-start.2 = (bf16[64,4,512]{2,1,0:T(4,128)(2,1)S(1)}, bf16[64,4,512]{2,1,0:T(4,128)(2,1)}, u32[]{:S(2)}) copy-start(bf16[64,4,512]{2,1,0:T(4,128)(2,1)} %reshape.94) | copy-start | bytes 786436
  279.9 0.9 copy-start.4
  291.5 9.4 %all-to-all-start.3 = ((bf16[32,2,2048]{2,0,1:T(8,128)(2,1)}), bf16[32,2,2048]{2,0,1:T(8,128)(2,1)}, u32[]{:S(2)}, u32[]{:S(2)}) async-start(bf16[32,2,2048]{2,0,1:T(8,128)(2,1)} %copy.80), calls=%async_computation.3 | async-start | bytes 524288 | tf_op jit(solution)/shard_map/all_to_all | solution.py:47
  300.9 9.4 %all-to-all-start.7 = ((bf16[32,2,2048]{2,0,1:T(8,128)(2,1)}), bf16[32,2,2048]{2,0,1:T(8,128)(2,1)}, u32[]{:S(2)}, u32[]{:S(2)}) async-start(bf16[32,2,2048]{2,0,1:T(8,128)(2,1)} %copy.101), calls=%async_computation.7 | async-start | bytes 524288 | tf_op jit(solution)/shard_map/all_to_all | solution.py:47
  425.5 25.6 %slice-start.6 = ((s8[6291456]{0:T(1024)(128)(4,1)}), s8[2097152]{0:T(1024)(128)(4,1)S(1)}, s32[]{:S(2)}) async-start(s8[6291456]{0:T(1024)(128)(4,1)} %bitcast.118), calls=%async_computation.17 | async-start | bytes 4194304
  444.4 6.7 %slice-start.7 = ((s8[6291456]{0:T(1024)(128)(4,1)}), s8[4194304]{0:T(1024)(128)(4,1)S(1)}, s32[]{:S(2)}) async-start(s8[6291456]{0:T(1024)(128)(4,1)} %bitcast.118), calls=%async_computation.18 | async-start | bytes 8388608
  444.4 6.7 %copy-start = (f32[4,3,256,256]{3,2,1,0:T(8,128)S(1)}, f32[4,3,256,256]{3,2,1,0:T(8,128)}, u32[]{:S(2)}) copy-start(f32[4,3,256,256]{3,2,1,0:T(8,128)} %get-tuple-element.22) | copy-start | bytes 9437188
  444.4 33.2 %slice-start = ((s8[6291456]{0:T(1024)(128)(4,1)}), s8[4194304]{0:T(1024)(128)(4,1)S(1)}, s32[]{:S(2)}) async-start(s8[6291456]{0:T(1024)(128)(4,1)} %bitcast.112), calls=%async_computation.11 | async-start | bytes 8388608
  451.1 26.4 %slice-start.1 = ((s8[6291456]{0:T(1024)(128)(4,1)}), s8[2097152]{0:T(1024)(128)(4,1)S(1)}, s32[]{:S(2)}) async-start(s8[6291456]{0:T(1024)(128)(4,1)} %bitcast.112), calls=%async_computation.12 | async-start | bytes 4194304
  477.6 6.6 %copy-start.6 = (bf16[64,4,512]{2,1,0:T(4,128)(2,1)S(1)}, bf16[64,4,512]{2,1,0:T(4,128)(2,1)}, u32[]{:S(2)}) copy-start(bf16[64,4,512]{2,1,0:T(4,128)(2,1)} %reshape.95) | copy-start | bytes 786436
  484.1 4.7 copy-start.3
Sparse Core Ops, SparseCore 0:
  9.5 64.1 all-gather.1
  82.7 137.9 all-reduce.2
  286.1 139.3 all-reduce.4
where the time goes:
time: 502 us; the launch traced here: 497 us
  waiting for transfers between devices  285 us (57%)
  matrix products  130 us (26%)
  starting transfers between devices  29.8 us (6%)
  local copies, waits for them, and re-layouts  26.7 us (5%)
  between operations  14.1 us (3%)
  other arithmetic  11.8 us (2%)
    psum x2, waiting for transfers between devices, local(): total_grad = lax.psum(gradients, 'seq')  219 us
    dot_general x4, matrix products, local_gram(): jnp.einsum('hmrf,hmrg->hmfg', weight_matrices, weight_matrices, precision...  59.2 us
    all_gather x1, waiting for transfers between devices, local(): weights = lax.all_gather(fast_init, 'seq', axis=2, tiled=True)  38.2 us
    dot_general x4, matrix products, newton_schulz(): jnp.einsum('hmrf,hmfg->hmrg', current_weights, polynomial_update, precisi...  36.9 us
    dot_general x4, matrix products, newton_schulz(): jnp.einsum('hmfg,hmgk->hmfk', gram_matrix, gram_matrix, precision=FULL_PR...  21.1 us
  transfers between devices with their start and end apart: 11, of which 11 were waited for; matrix products, arithmetic and copies ran while one was open for 5% of the time, Pallas kernels for 0%

commit v1 on v0

--- a/solution.py
+++ b/solution.py
@@ -43,9 +43,17 @@
     head_size = weights.shape[2]
     results = []
     for group_index in range(queries.shape[0]):
+
+        def keep_up_set(frame_in, along_axis):
+            e_next = lax.axis_size(along_axis)
+            val2 = jnp.split(frame_in, e_next, axis=1)
+            row_out = jnp.stack(val2, axis=0)
+            value_now = lax.all_to_all(row_out, along_axis, split_axis=0, concat_axis=0)
+            return jnp.concatenate(value_now, axis=0)
+
         query_flat, key_flat, value_flat, rate_rows = (
             lax.all_to_all(queries[group_index], "head", split_axis=1, concat_axis=0, tiled=True),
-            lax.all_to_all(keys[group_index], "head", split_axis=1, concat_axis=0, tiled=True),
+            keep_up_set(keys[group_index], "head"),
             lax.all_to_all(values[group_index], "head", split_axis=1, concat_axis=0, tiled=True),
             lax.all_to_all(rates[group_index], "head", split_axis=1, concat_axis=0, tiled=True),
         )

time: 502 us -> 492 us (0.980)
  matrix products: 130 us -> 116 us
    dot_general x4, matrix products: 36.9 us -> 28.9 us  [newton_schulz(): jnp.einsum('hmrf,hmfg->hmrg', current_weights, polynomial_update, precisi...]
    dot_general x4, matrix products: 59.2 us -> 53.3 us  [local_gram(): jnp.einsum('hmrf,hmrg->hmfg', weight_matrices, weight_matrices, precision...]
where the time goes in v1:
time: 492 us; the launch traced here: 483 us
  waiting for transfers between devices  285 us (58%)
  matrix products  116 us (24%)
  starting transfers between devices  29.5 us (6%)
  local copies, waits for them, and re-layouts  24.9 us (5%)
  between operations  13.9 us (3%)
  other arithmetic  13.5 us (3%)
    psum x2, waiting for transfers between devices, local(): total_grad = lax.psum(gradients, 'seq')  220 us
    dot_general x4, matrix products, local_gram(): jnp.einsum('hmrf,hmrg->hmfg', weight_matrices, weight_matrices, precision...  53.3 us
    all_gather x1, waiting for transfers between devices, local(): weights = lax.all_gather(fast_init, 'seq', axis=2, tiled=True)  38.4 us
    dot_general x4, matrix products, newton_schulz(): jnp.einsum('hmrf,hmfg->hmrg', current_weights, polynomial_update, precisi...  28.9 us
    dot_general x4, matrix products, newton_schulz(): jnp.einsum('hmfg,hmgk->hmfk', gram_matrix, gram_matrix, precision=FULL_PR...  21.5 us
    all_to_all x2, waiting for transfers between devices, local(): lax.all_to_all(values[group_index], 'head', split_axis=1, concat_axis=0,...  10.1 us
  transfers between devices with their start and end apart: 11, of which 11 were waited for; matrix products, arithmetic and copies ran while one was open for 5% of the time, Pallas kernels for 0%

profile of v1, /device:TPU:0, one launch (start us, length us, event | category | flops | bytes accessed | tf_op | source)
XLA Modules:
  0.0 483.2 jit_solution(17130723074519323378)
XLA Ops:
  9.7 4.3 all-to-all-start.1
  17.7 3.5 all-to-all-start.2
  21.3 5.1 %all-to-all-done.2 = bf16[32,2,2048]{2,0,1:T(8,128)(2,1)S(1)} async-done(((bf16[32,2,2048]{2,0,1:T(8,128)(2,1)}), bf16[32,2,2048]{2,0,1:T(8,128)(2,1)S(1)}, u32[]{:S(2)}, u32[]{:S(2)}) %all-to-all-start.2) | async-done | bytes 262176 | tf_op jit(solution)/shard_map/all_to_all | solution.py:57
  26.3 3.4 all-to-all-start
  30.3 4.7 all-to-all-done
  35.3 38.4 %all-gather.2.cloned.1.call-done = f32[4,3,512,256]{3,2,0,1:T(8,128)} async-done(((f32[4,3,32,256]{3,2,0,1:T(8,128)}), f32[4,3,512,256]{3,2,0,1:T(8,128)}) %all-gather.2.cloned.1.call-update) | async-done | bytes 6291472 | tf_op jit(solution)/shard_map/all_gather | solution.py:41
  73.7 3.1 convert_element_type.105
  79.3 3.4 pad_maximum_fusion
  82.7 3.2 all-to-all-start.5
  89.5 3.4 all-to-all-start.6
  93.1 5.1 %all-to-all-done.6 = bf16[32,2,2048]{2,0,1:T(8,128)(2,1)S(1)} async-done(((bf16[32,2,2048]{2,0,1:T(8,128)(2,1)}), bf16[32,2,2048]{2,0,1:T(8,128)(2,1)S(1)}, u32[]{:S(2)}, u32[]{:S(2)}) %all-to-all-start.6) | async-done | bytes 262176 | tf_op jit(solution)/shard_map/all_to_all | solution.py:57
  98.1 3.4 all-to-all-start.4
  102.0 4.7 all-to-all-done.4
  108.5 112.3 %all-reduce.3.cloned.1.call-done = f32[4,3,512,256]{3,2,0,1:T(8,128)} async-done(((f32[4,3,512,256]{3,2,0,1:T(8,128)}), f32[4,3,512,256]{3,2,0,1:T(8,128)}) %all-reduce.3.cloned.1.call-update) | async-done | bytes 6291472 | tf_op jit(solution)/shard_map/psum | solution.py:89
  220.8 15.8 %select_reduce_fusion.1 = (f32[4,3]{1,0:T(4,128)S(1)}, f32[4,3,256,256]{3,2,1,0:T(8,128)}) fusion(pred[256,256]{1,0:T(8,128)(4,1)S(1)} %iota_compare_fusion, f32[4,3,512,256]{3,2,0,1:T(8,128)} %all-reduce.3.cloned.1.call-done), kind=kOutput, calls=%fused_computation.31 | convolution fusion | flops 4833411072 | bytes 9502768 | tf_op jit(solution)/shard_map/hmrf,hmrg->hmfg/dot_general | solution.py:20
  236.8 6.4 %fusion.36 = f32[4,3,256,256]{3,2,1,0:T(8,128)S(1)} fusion(f32[4,3,256,256]{3,2,1,0:T(8,128)} %get-tuple-element.22, f32[4,3]{1,0:T(4,128)S(1)} %get-tuple-element.19), kind=kOutput, calls=%fused_computation.46 | convolution fusion | flops 2416705536 | bytes 6291504 | tf_op jit(solution)/shard_map/hmfg,hmgk->hmfk/dot_general | solution.py:32
  243.2 6.7 %fusion.10 = f32[4,3,512,256]{3,2,1,0:T(8,128)S(1)} fusion(f32[4,3,256,256]{3,2,1,0:T(8,128)S(1)} %fusion.36, f32[256,256]{1,0:T(8,128)S(1)} %broadcast_select_fusion, f32[4,3,256,256]{3,2,1,0:T(8,128)S(1)} %copy-done.1, f32[4,3]{1,0:T(4,128)S(1)} %get-tuple-element.19, f32[4,3,512,256]{3,2,0,1:T(8,128)S(1)} %bitcast.119, f32[4,3]{0,1:T(4,128)S(1)} %copy.68), kind=kOutput, calls=%fused_computation.12 | convolution fusion | flops 4837343232 | bytes 19136608 | tf_op jit(solution)/shard_map/hmrf,hmfg->hmrg/dot_general | solution.py:34
  249.9 10.6 %fusion.100 = f32[4,3,256,256]{3,2,1,0:T(8,128)S(1)} fusion(f32[4,3,512,256]{3,2,1,0:T(8,128)S(1)} %fusion.10), kind=kOutput, calls=%fused_computation.152 | convolution fusion | flops 4831838208 | bytes 9437184 | tf_op jit(solution)/shard_map/hmrf,hmrg->hmfg/dot_general | solution.py:20
  260.6 4.0 multiply_add_fusion.1
  264.7 8.1 %fusion.99 = (bf16[4,3,512,256]{3,2,0,1:T(8,128)(2,1)S(1)}, f32[4,3,512,256]{3,2,0,1:T(8,128)}) fusion(f32[4,3,512,256]{3,2,0,1:T(8,128)S(1)} %bitcast.117, f32[4,3,256,256]{3,2,1,0:T(8,128)S(1)} %multiply_add_fusion.1, f32[4,3,512,256]{3,2,1,0:T(8,128)S(1)} %fusion.10), kind=kOutput, calls=%fused_computation.151 | convolution fusion | flops 4836556800 | bytes 25165824 | tf_op jit(solution)/shard_map/hmrf,hmfg->hmrg/dot_general | solution.py:34
  275.5 3.4 pad_maximum_fusion.1
  284.4 4.1 all-to-all-start.3
  293.8 4.1 all-to-all-start.7
  299.7 3.4 all-to-all-done.7
  311.4 107.2 %all-reduce.5.cloned.1.call-done = f32[4,3,512,256]{3,2,0,1:T(8,128)} async-done(((f32[4,3,512,256]{3,2,0,1:T(8,128)}), f32[4,3,512,256]{3,2,0,1:T(8,128)}) %all-reduce.5.cloned.1.call-update) | async-done | bytes 6291472 | tf_op jit(solution)/shard_map/psum | solution.py:89
  418.6 16.1 %select_reduce_fusion = (f32[4,3]{1,0:T(4,128)S(1)}, f32[4,3,256,256]{3,2,1,0:T(8,128)}) fusion(pred[256,256]{1,0:T(8,128)(4,1)S(1)} %iota_compare_fusion, f32[4,3,512,256]{3,2,0,1:T(8,128)} %all-reduce.5.cloned.1.call-done), kind=kOutput, calls=%fused_computation.24 | convolution fusion | flops 4833411072 | bytes 9502768 | tf_op jit(solution)/shard_map/hmrf,hmrg->hmfg/dot_general | solution.py:20
  434.8 6.7 %fusion.37 = f32[4,3,256,256]{3,2,1,0:T(8,128)S(1)} fusion(f32[4,3,256,256]{3,2,1,0:T(8,128)} %get-tuple-element.26, f32[4,3]{1,0:T(4,128)S(1)} %get-tuple-element.17), kind=kOutput, calls=%fused_computation.47 | convolution fusion | flops 2416705536 | bytes 6291504 | tf_op jit(solution)/shard_map/hmfg,hmgk->hmfk/dot_general | solution.py:32
  441.5 7.6 %fusion.8 = f32[4,3,512,256]{3,2,1,0:T(8,128)S(1)} fusion(f32[4,3,256,256]{3,2,1,0:T(8,128)S(1)} %fusion.37, f32[256,256]{1,0:T(8,128)S(1)} %broadcast_select_fusion, f32[4,3,256,256]{3,2,1,0:T(8,128)S(1)} %copy-done, f32[4,3]{1,0:T(4,128)S(1)} %get-tuple-element.17, f32[4,3,512,256]{3,2,0,1:T(8,128)S(1)} %bitcast.121, f32[4,3]{0,1:T(4,128)S(1)} %copy.87), kind=kOutput, calls=%fused_computation.10 | convolution fusion | flops 4837343232 | bytes 19136608 | tf_op jit(solution)/shard_map/hmrf,hmfg->hmrg/dot_general | solution.py:34
  449.1 10.7 %fusion.101 = f32[4,3,256,256]{3,2,1,0:T(8,128)S(1)} fusion(f32[4,3,512,256]{3,2,1,0:T(8,128)S(1)} %fusion.8), kind=kOutput, calls=%fused_computation.153 | convolution fusion | flops 4831838208 | bytes 9437184 | tf_op jit(solution)/shard_map/hmrf,hmrg->hmfg/dot_general | solution.py:20
  459.9 4.3 multiply_add_fusion
  464.2 6.5 %subtract_convert_fusion = bf16[4,3,512,256]{3,2,0,1:T(8,128)(2,1)S(1)} fusion(f32[4,3,512,256]{3,2,0,1:T(8,128)S(1)} %bitcast.115, f32[4,3,256,256]{3,2,1,0:T(8,128)S(1)} %multiply_add_fusion, f32[4,3,512,256]{3,2,1,0:T(8,128)S(1)} %fusion.8), kind=kOutput, calls=%fused_computation.14 | convolution fusion | flops 4836556800 | bytes 18874368 | tf_op jit(solution)/shard_map/hmrf,hmfg->hmrg/dot_general | solution.py:34
  471.8 2.4 fusion.39
  (99 shorter events, 43.0 us)
Async XLA Ops:
  6.5 8.5 %copy-start.5 = (bf16[2,32,4096]{2,1,0:T(8,128)(2,1)S(1)}, bf16[2,32,4096]{2,1,0:T(8,128)(2,1)}, u32[]{:S(2)}) copy-start(bf16[2,32,4096]{2,1,0:T(8,128)(2,1)} %param.7) | copy-start | bytes 1572868
  6.5 67.2 %all-gather.2.cloned.1.call-start = ((), (), s32[]{:S(2)}) async-start(), calls=%async_computation.8 | async-start | bytes 6684672 | tf_op jit(solution)/shard_map/all_gather | solution.py:41
  9.7 8.0 %all-to-all-start.1 = ((bf16[32,2,4]{0,2,1:T(4,128)(2,1)}), bf16[32,2,4]{0,2,1:T(4,128)(2,1)S(1)}, u32[]{:S(2)}, u32[]{:S(2)}) async-start(bf16[32,2,4]{0,2,1:T(4,128)(2,1)} %bitcast.3), calls=%async_computation.1 | async-start | bytes 4096 | tf_op jit(solution)/shard_map/all_to_all | solution.py:58
  17.7 8.6 %all-to-all-start.2 = ((bf16[32,2,2048]{2,0,1:T(8,128)(2,1)}), bf16[32,2,2048]{2,0,1:T(8,128)(2,1)S(1)}, u32[]{:S(2)}, u32[]{:S(2)}) async-start(bf16[32,2,2048]{2,0,1:T(8,128)(2,1)} %copy.59), calls=%async_computation.2 | async-start | bytes 524288 | tf_op jit(solution)/shard_map/all_to_all | solution.py:57
  26.3 8.6 %all-to-all-start = ((bf16[2,32,2048]{2,1,0:T(8,128)(2,1)}), bf16[2,32,2048]{2,1,0:T(8,128)(2,1)S(1)}, u32[]{:S(2)}, u32[]{:S(2)}) async-start(bf16[2,32,2048]{2,1,0:T(8,128)(2,1)} %pad_maximum_fusion.3), calls=%async_computation | async-start | bytes 524288 | tf_op jit(solution)/shard_map/all_to_all | solution.py:51
  29.8 191.0 %all-reduce.3.cloned.1.call-start = ((), (), s32[]{:S(2)}) async-start(), calls=%async_computation.9 | async-start | bytes 12582912 | tf_op jit(solution)/shard_map/psum | solution.py:89
  82.7 6.8 %all-to-all-start.5 = ((bf16[32,2,4]{0,2,1:T(4,128)(2,1)}), bf16[32,2,4]{0,2,1:T(4,128)(2,1)S(1)}, u32[]{:S(2)}, u32[]{:S(2)}) async-start(bf16[32,2,4]{0,2,1:T(4,128)(2,1)} %bitcast.26), calls=%async_computation.5 | async-start | bytes 4096 | tf_op jit(solution)/shard_map/all_to_all | solution.py:58
  89.5 8.6 %all-to-all-start.6 = ((bf16[32,2,2048]{2,0,1:T(8,128)(2,1)}), bf16[32,2,2048]{2,0,1:T(8,128)(2,1)S(1)}, u32[]{:S(2)}, u32[]{:S(2)}) async-start(bf16[32,2,2048]{2,0,1:T(8,128)(2,1)} %copy.78), calls=%async_computation.6 | async-start | bytes 524288 | tf_op jit(solution)/shard_map/all_to_all | solution.py:57
  98.1 8.6 %all-to-all-start.4 = ((bf16[2,32,2048]{2,1,0:T(8,128)(2,1)}), bf16[2,32,2048]{2,1,0:T(8,128)(2,1)S(1)}, u32[]{:S(2)}, u32[]{:S(2)}) async-start(bf16[2,32,2048]{2,1,0:T(8,128)(2,1)} %pad_maximum_fusion.4), calls=%async_computation.4 | async-start | bytes 524288 | tf_op jit(solution)/shard_map/all_to_all | solution.py:51
  101.6 317.0 %all-reduce.5.cloned.1.call-start = ((), (), s32[]{:S(2)}) async-start(), calls=%async_computation.10 | async-start | bytes 12582912 | tf_op jit(solution)/shard_map/psum | solution.py:89
  220.8 22.4 %slice-start.4 = ((s8[6291456]{0:T(1024)(128)(4,1)}), s8[2097152]{0:T(1024)(128)(4,1)S(1)}, s32[]{:S(2)}) async-start(s8[6291456]{0:T(1024)(128)(4,1)} %bitcast.118), calls=%async_computation.15 | async-start | bytes 4194304
  236.8 6.4 %slice-start.5 = ((s8[6291456]{0:T(1024)(128)(4,1)}), s8[4194304]{0:T(1024)(128)(4,1)S(1)}, s32[]{:S(2)}) async-start(s8[6291456]{0:T(1024)(128)(4,1)} %bitcast.118), calls=%async_computation.16 | async-start | bytes 8388608
  236.8 6.4 %copy-start.1 = (f32[4,3,256,256]{3,2,1,0:T(8,128)S(1)}, f32[4,3,256,256]{3,2,1,0:T(8,128)}, u32[]{:S(2)}) copy-start(f32[4,3,256,256]{3,2,1,0:T(8,128)} %get-tuple-element.22) | copy-start | bytes 9437188
  236.8 27.9 %slice-start.2 = ((s8[6291456]{0:T(1024)(128)(4,1)}), s8[4194304]{0:T(1024)(128)(4,1)S(1)}, s32[]{:S(2)}) async-start(s8[6291456]{0:T(1024)(128)(4,1)} %bitcast.116), calls=%async_computation.13 | async-start | bytes 8388608
  243.2 21.4 %slice-start.3 = ((s8[6291456]{0:T(1024)(128)(4,1)}), s8[2097152]{0:T(1024)(128)(4,1)S(1)}, s32[]{:S(2)}) async-start(s8[6291456]{0:T(1024)(128)(4,1)} %bitcast.116), calls=%async_computation.14 | async-start | bytes 4194304
  264.7 8.1 %copy-start.2 = (bf16[64,4,512]{2,1,0:T(4,128)(2,1)S(1)}, bf16[64,4,512]{2,1,0:T(4,128)(2,1)}, u32[]{:S(2)}) copy-start(bf16[64,4,512]{2,1,0:T(4,128)(2,1)} %reshape_reshape.7) | copy-start | bytes 786436
  272.8 0.9 copy-start.4
  284.4 9.4 %all-to-all-start.3 = ((bf16[32,2,2048]{2,0,1:T(8,128)(2,1)}), bf16[32,2,2048]{2,0,1:T(8,128)(2,1)}, u32[]{:S(2)}, u32[]{:S(2)}) async-start(bf16[32,2,2048]{2,0,1:T(8,128)(2,1)} %copy.72), calls=%async_computation.3 | async-start | bytes 524288 | tf_op jit(solution)/shard_map/all_to_all | solution.py:55
  293.8 9.4 %all-to-all-start.7 = ((bf16[32,2,2048]{2,0,1:T(8,128)(2,1)}), bf16[32,2,2048]{2,0,1:T(8,128)(2,1)}, u32[]{:S(2)}, u32[]{:S(2)}) async-start(bf16[32,2,2048]{2,0,1:T(8,128)(2,1)} %copy.91), calls=%async_computation.7 | async-start | bytes 524288 | tf_op jit(solution)/shard_map/all_to_all | solution.py:55
  418.6 22.9 %slice-start.6 = ((s8[6291456]{0:T(1024)(128)(4,1)}), s8[2097152]{0:T(1024)(128)(4,1)S(1)}, s32[]{:S(2)}) async-start(s8[6291456]{0:T(1024)(128)(4,1)} %bitcast.120), calls=%async_computation.17 | async-start | bytes 4194304
  434.8 6.7 %slice-start.7 = ((s8[6291456]{0:T(1024)(128)(4,1)}), s8[4194304]{0:T(1024)(128)(4,1)S(1)}, s32[]{:S(2)}) async-start(s8[6291456]{0:T(1024)(128)(4,1)} %bitcast.120), calls=%async_computation.18 | async-start | bytes 8388608
  434.8 6.7 %copy-start = (f32[4,3,256,256]{3,2,1,0:T(8,128)S(1)}, f32[4,3,256,256]{3,2,1,0:T(8,128)}, u32[]{:S(2)}) copy-start(f32[4,3,256,256]{3,2,1,0:T(8,128)} %get-tuple-element.26) | copy-start | bytes 9437188
  434.8 29.4 %slice-start = ((s8[6291456]{0:T(1024)(128)(4,1)}), s8[4194304]{0:T(1024)(128)(4,1)S(1)}, s32[]{:S(2)}) async-start(s8[6291456]{0:T(1024)(128)(4,1)} %bitcast.114), calls=%async_computation.11 | async-start | bytes 8388608
  441.5 22.7 %slice-start.1 = ((s8[6291456]{0:T(1024)(128)(4,1)}), s8[2097152]{0:T(1024)(128)(4,1)S(1)}, s32[]{:S(2)}) async-start(s8[6291456]{0:T(1024)(128)(4,1)} %bitcast.114), calls=%async_computation.12 | async-start | bytes 4194304
  464.2 6.6 %copy-start.6 = (bf16[64,4,512]{2,1,0:T(4,128)(2,1)S(1)}, bf16[64,4,512]{2,1,0:T(4,128)(2,1)}, u32[]{:S(2)}) copy-start(bf16[64,4,512]{2,1,0:T(4,128)(2,1)} %reshape.77) | copy-start | bytes 786436
  470.8 4.7 copy-start.3
Sparse Core Ops, SparseCore 0:
  9.5 64.1 all-gather.1
  82.8 137.9 all-reduce.2
  279.0 139.5 all-reduce.4
